TPU v7x, 32 devices: a whole 2x2x4 slice. The times are simulated.
32 devices in a mesh: dir: 2 (over x), gz: 8 (over z, y), gy: 2 (over core).
Axes of the slice: x: 2, y: 2, z: 4, core: 2. Of those that a mesh axis runs over, the one named last changes fastest.
Arguments:
- estimate: bfloat16 [96, 64, 128, 128], P('dir', 'gz', 'gy'), may hold values from -6 to 6
- observed: bfloat16 [96, 64, 128, 128], P('dir', 'gz', 'gy'), may hold values from -6 to 6
- profile_weight: float32 [17], replicated, may hold values from 0.02 to 0.12
- band_offset: int32 [17], replicated, may hold values from -8 to 8, as said below
- slab_shot: int32 [8], replicated, may hold values from 0 to 3
- shot_gain: float32 [4, 96], P(None, 'dir'), may hold values from 0.1 to 1.9
- fit_matrix: bfloat16 [96, 45], replicated, may hold values from -0.625 to 0.625
- basis: bfloat16 [45, 96], replicated, may hold values from -0.875 to 0.875
Outputs:
- correction: bfloat16 [96, 64, 128, 128], P('dir', 'gz', 'gy')
- updated: bfloat16 [96, 64, 128, 128], P('dir', 'gz', 'gy')
Inputs may be any that keep to these rules, and one draw needn't show every extreme that they name: `band_offset`: the first tap's offset is -8 and the last tap's is 8.
All inputs are finite; a program needn't handle non-finite values.
Results may differ from a plain program's by a relative error of at most 0.0055.
Values may be sent and summed in bfloat16 or wider, within the bound.
A program may use at most 128 MiB of HBM per device.

v0:
```python
import functools

import jax
import jax.numpy as jnp
from jax import lax
from jax.experimental import pallas as pl
from jax.experimental.pallas import tpu as pltpu
from jax.sharding import PartitionSpec as P

SLAB = 8
STEP_SIZE = 0.5
ROWS = 8
PIECES = 4
CUTS = 2
MESH = pl.DeviceIdType.MESH

def divisor(count, most):
    return max(size for size in range(1, most + 1) if count % size == 0)


def iota(shape, axis):
    return lax.broadcasted_iota(jnp.int32, shape, axis)


def ones_where(hit):
    return jnp.where(hit, 1.0, 0.0).astype(jnp.bfloat16)


def against(a, b):
    return lax.dot_general(a, b, (((1,), (1,)), ((), ())), preferred_element_type=jnp.float32)


def same_row(shape):
    return lax.rem(iota(shape, 0), ROWS) == lax.rem(iota(shape, 1), ROWS)


def band_matrix(weight, offset, odd, depth, sign):
    shape = (2 * depth * ROWS, 4 * depth * ROWS)
    at, source = iota(shape, 0) // ROWS, iota(shape, 1) // ROWS

    def place(block):
        return block + odd * (3 - 2 * block)

    gap = place(source // depth) * depth + lax.rem(source, depth)
    gap = sign * (gap - place(1 + at // depth) * depth - lax.rem(at, depth))
    total = jnp.zeros(shape, jnp.float32)
    for tap in range(weight.shape[0]):
        total = total + jnp.where(gap == offset[tap], weight[tap], 0.0)
    total = jnp.where(same_row(shape), total, 0.0)
    high = total.astype(jnp.bfloat16)
    low = (total - high.astype(jnp.float32)).astype(jnp.bfloat16)
    return jnp.concatenate([high, low], axis=0)


def exchange_kernel(
    sizes, est, obs, weight, offset, shot, gain, fit, out,
    est_kept, obs_kept, est_got, obs_got, far_a, far_b, res, band, band_back, fit_wide, own,
    part_out, part_in, coef, coef_a, coef_b, mine, other, returned,
    load_sem, store_sem, pair_sem, far_sem, part_sem, edge_sem, back_sem, ret_sem,
):
    parts, slabs, chunks, dirs, depth, width, share = sizes
    slab = lax.axis_index("gz").astype(jnp.int32)
    part = lax.axis_index("dir").astype(jnp.int32)
    odd = lax.rem(slab, 2)
    partner = slab + 1 - 2 * odd
    away = slab - 2 + 4 * odd
    across = slab + 2 - 4 * odd
    has_away = jnp.logical_and(away >= 0, away < slabs)
    has_across = jnp.logical_and(across >= 0, across < slabs)
    some = dirs // CUTS
    span = share * ROWS
    count = divisor(share // 2, PIECES)
    step = span // count
    pair_rows = 2 * ROWS
    half = depth * ROWS

    def part_of(hop):
        return lax.rem(part + hop, parts)

    barrier = pltpu.get_barrier_semaphore()

    def greet(name, index):
        pl.semaphore_signal(barrier, inc=1, device_id={name: index}, device_id_type=MESH)

    greet("gz", partner)
    for hop in range(1, parts):
        greet("dir", part_of(hop))

    @pl.when(has_away)
    def _():
        greet("gz", away)

    @pl.when(has_across)
    def _():
        greet("gz", across)

    pl.semaphore_wait(barrier, parts + has_away.astype(jnp.int32) + has_across.astype(jnp.int32))

    def remote(source, target, sems, name, index):
        return pltpu.make_async_remote_copy(
            src_ref=source, dst_ref=target, send_sem=sems.at[0], recv_sem=sems.at[1],
            device_id={name: index}, device_id_type=MESH,
        )

    def rows_at(side, chunk):
        return pl.ds(pl.multiple_of((side * chunks + chunk) * ROWS, ROWS), ROWS)

    def cut_of(cut):
        return pl.ds(cut * some, some)

    def piece(i):
        return pl.ds(i * step, step)

    def pair_copy(kind, chunk, cut):
        source, target = ((est, est_got), (obs, obs_got))[kind]
        return remote(
            source.at[cut_of(cut), :, rows_at(1 - odd, chunk), :],
            target.at[chunk, cut_of(cut)],
            pair_sem.at[kind, chunk, cut], "gz", partner,
        )

    def away_copy(chunk, cut):
        return remote(
            est.at[cut_of(cut), :, rows_at(odd, chunk), :],
            far_a.at[chunk, cut_of(cut)],
            far_sem.at[0, chunk, cut], "gz", away,
        )

    def across_copy(chunk, cut):
        return remote(
            est_got.at[chunk, cut_of(cut)], far_b.at[chunk, cut_of(cut)],
            far_sem.at[1, chunk, cut], "gz", across,
        )

    def load_copy(kind, chunk):
        source, target = ((est, est_kept), (obs, obs_kept))[kind]
        return pltpu.make_async_copy(
            source.at[:, :, rows_at(odd, chunk), :], target.at[chunk], load_sem.at[kind, chunk]
        )

    def part_copy(chunk, hop, i):
        return remote(
            part_out.at[chunk, hop - 1, :, piece(i), :], part_in.at[chunk, hop - 1, :, piece(i), :],
            part_sem.at[chunk, hop - 1, i], "dir", part_of(hop),
        )

    def edge_copy(kind, chunk, i):
        target, index = ((coef_a, away), (coef_b, across))[kind]
        return remote(
            coef.at[chunk, pl.ds(kind * depth, depth), piece(i), :],
            target.at[chunk, :, piece(i), :],
            edge_sem.at[kind, chunk, i], "gz", index,
        )

    def back_copy(chunk, i):
        return remote(
            other.at[chunk, :, piece(i), :], returned.at[chunk, :, piece(i), :],
            back_sem.at[chunk, i], "gz", partner,
        )

    def tile_of(kind, chunk):
        side = odd if kind == 0 else 1 - odd
        return side * chunks + chunk

    def ret_copy(kind, chunk, hop, i):
        source = (mine, returned)[kind]
        return remote(
            source.at[chunk, :, piece(i), :], out.at[tile_of(kind, chunk), part, :, piece(i), :],
            ret_sem.at[kind, chunk, hop - 1, i], "dir", part_of(hop),
        )

    def store_copy(kind, chunk):
        source = (mine, returned)[kind]
        return pltpu.make_async_copy(
            source.at[chunk], out.at[tile_of(kind, chunk), part], store_sem.at[kind, chunk]
        )

    def begin(chunk):
        for kind in range(2):
            for cut in range(CUTS):
                pair_copy(kind, chunk, cut).start()

        @pl.when(has_away)
        def _():
            for cut in range(CUTS):
                away_copy(chunk, cut).start()

        for kind in range(2):
            load_copy(kind, chunk).start()

    def forward(chunk, cut):
        pair_copy(0, chunk, cut).wait_recv()

        @pl.when(has_across)
        def _():
            across_copy(chunk, cut).start()

    def arrive(near, far):
        @pl.when(has_across)
        def _():
            near.wait_recv()

        @pl.when(has_away)
        def _():
            far.wait_recv()

    shots = [shot[lax.div(index * depth, SLAB)] for index in (slab, partner)]

    def residual(chunk, cut):
        arrive(away_copy(chunk, cut), across_copy(chunk, cut))
        pair_copy(1, chunk, cut).wait_recv()

        def one(j, carry):
            d = cut * some + 2 * j
            columns = []
            for e in range(2):
                planes = [
                    ref[chunk, d + e].astype(jnp.float32).reshape(half, width)
                    for ref in (far_b, est_kept, est_got, far_a)
                ]
                columns.append(jnp.concatenate(planes, axis=0))
            wide = jnp.concatenate(columns, axis=1).astype(jnp.bfloat16)
            sums = jnp.dot(band[...], wide, preferred_element_type=jnp.float32)
            sums = sums[: 2 * half] + sums[2 * half :]
            for o, seen in enumerate((obs_kept, obs_got)):
                values = []
                for e in range(2):
                    scale = gain[shots[o], d + e]
                    blurred = sums[o * half : (o + 1) * half, e * width : (e + 1) * width]
                    value = seen[chunk, d + e].astype(jnp.float32).reshape(half, width)
                    values.append(scale * (value - scale * blurred))
                at = pl.ds(pl.multiple_of(d * ROWS, pair_rows), pair_rows)
                for z in range(depth):
                    cut_rows = slice(z * ROWS, (z + 1) * ROWS)
                    both = jnp.concatenate([value[cut_rows] for value in values], axis=0)
                    res[o * depth + z, at, :] = both.astype(jnp.bfloat16)
            return carry

        lax.fori_loop(0, some // 2, one, 0)

    def fitting(chunk):
        def one(j, carry):
            z = 2 * j
            wide = jnp.concatenate([res[z], res[z + 1]], axis=1)
            made = jnp.dot(fit_wide[...], wide, preferred_element_type=jnp.float32)
            for e in range(2):
                value = made[:, e * width : (e + 1) * width]
                own[z + e] = value[:span]
                for hop in range(1, parts):
                    piece_of = value[hop * span : (hop + 1) * span]
                    part_out[chunk, hop - 1, z + e] = piece_of.astype(jnp.bfloat16)
            return carry

        lax.fori_loop(0, depth, one, 0)
        for i in range(count):
            for hop in range(1, parts):
                part_copy(chunk, hop, i).start()

    def gather(chunk, i):
        for hop in range(1, parts):
            part_copy(chunk, hop, i).wait_recv()

        def one(z, carry):
            value = own[z, piece(i), :]
            for hop in range(1, parts):
                value = value + part_in[chunk, hop - 1, z, piece(i), :].astype(jnp.float32)
            coef[chunk, z, piece(i), :] = value.astype(jnp.bfloat16)
            return carry

        lax.fori_loop(0, 2 * depth, one, 0)

        @pl.when(has_away)
        def _():
            edge_copy(0, chunk, i).start()

        @pl.when(has_across)
        def _():
            edge_copy(1, chunk, i).start()

    def smooth(chunk, i):
        arrive(edge_copy(0, chunk, i), edge_copy(1, chunk, i))

        def one(j, carry):
            at = pl.ds(pl.multiple_of(i * step + j * pair_rows, pair_rows), pair_rows)
            planes = [coef_b[chunk, z, at, :] for z in range(depth)]
            planes += [coef[chunk, z, at, :] for z in range(2 * depth)]
            planes += [coef_a[chunk, z, at, :] for z in range(depth)]
            planes = [plane.astype(jnp.float32) for plane in planes]
            columns = [
                jnp.concatenate([plane[e * ROWS : (e + 1) * ROWS] for plane in planes], axis=0)
                for e in range(2)
            ]
            wide = jnp.concatenate(columns, axis=1).astype(jnp.bfloat16)
            sums = jnp.dot(band_back[...], wide, preferred_element_type=jnp.float32)
            sums = sums[: 2 * half] + sums[2 * half :]
            for o, ref in enumerate((mine, other)):
                for z in range(depth):
                    value = sums[o * half + z * ROWS : o * half + (z + 1) * ROWS]
                    both = jnp.concatenate([value[:, :width], value[:, width:]], axis=0)
                    ref[chunk, z, at, :] = both.astype(jnp.bfloat16)
            return carry

        lax.fori_loop(0, step // pair_rows, one, 0)
        back_copy(chunk, i).start()
        for hop in range(1, parts):
            ret_copy(0, chunk, hop, i).start()

    def pass_on(chunk, i):
        back_copy(chunk, i).wait_recv()
        for hop in range(1, parts):
            ret_copy(1, chunk, hop, i).start()

    begin(0)
    if chunks > 1:
        begin(1)

    nothing = jnp.zeros((dirs, depth, ROWS, width), jnp.bfloat16)
    no_coef = jnp.zeros((depth, span, width), jnp.bfloat16)

    def clear(ref, value):
        def one(chunk, carry):
            ref[chunk] = value
            return carry

        lax.fori_loop(0, chunks, one, 0)

    @pl.when(jnp.logical_not(has_across))
    def _():
        clear(far_a, nothing)
        clear(coef_a, no_coef)

    @pl.when(jnp.logical_not(has_away))
    def _():
        clear(far_b, nothing)
        clear(coef_b, no_coef)

    band[...] = band_matrix(weight, offset, odd, depth, 1)
    band_back[...] = band_matrix(weight, offset, odd, depth, -1)
    line = iota((parts * span, fit.shape[1]), 0) // ROWS
    chosen = lax.rem(line // share + part, parts) * share + lax.rem(line, share)
    spread = ones_where(chosen == iota(line.shape, 1))
    narrow = against(spread, fit[...]).astype(jnp.bfloat16)
    shape = (dirs * ROWS, fit.shape[0])
    spread = ones_where(iota(shape, 0) // ROWS + part * dirs == iota(shape, 1))
    full = against(narrow, spread)
    fit_wide[...] = jnp.where(same_row(full.shape), full, 0.0).astype(jnp.bfloat16)

    for cut in range(CUTS):
        forward(0, cut)
    for chunk in range(chunks):
        more = chunk + 1 < chunks
        for kind in range(2):
            load_copy(kind, chunk).wait()
        for cut in range(CUTS):
            residual(chunk, cut)
        fitting(chunk)
        if chunk:
            for i in range(count):
                pass_on(chunk - 1, i)
            store_copy(1, chunk - 1).start()
        for i in range(count):
            gather(chunk, i)
            for cut in range(CUTS):
                if more and cut * count // CUTS == i:
                    forward(chunk + 1, cut)
            if i:
                smooth(chunk, i - 1)
            if not more and i > 1:
                pass_on(chunk, i - 2)
        smooth(chunk, count - 1)
        store_copy(0, chunk).start()
        if not more:
            for i in range(max(count - 2, 0), count):
                pass_on(chunk, i)
            store_copy(1, chunk).start()
        if chunk + 2 < chunks:
            begin(chunk + 2)

    for chunk in range(chunks):
        for cut in range(CUTS):
            for kind in range(2):
                pair_copy(kind, chunk, cut).wait_send()

            @pl.when(has_away)
            def _(chunk=chunk, cut=cut):
                away_copy(chunk, cut).wait_send()

            @pl.when(has_across)
            def _(chunk=chunk, cut=cut):
                across_copy(chunk, cut).wait_send()

        for i in range(count):
            for hop in range(1, parts):
                part_copy(chunk, hop, i).wait_send()

            @pl.when(has_away)
            def _(chunk=chunk, i=i):
                edge_copy(0, chunk, i).wait_send()

            @pl.when(has_across)
            def _(chunk=chunk, i=i):
                edge_copy(1, chunk, i).wait_send()

            back_copy(chunk, i).wait_send()
            for kind in range(2):
                for hop in range(1, parts):
                    ret_copy(kind, chunk, hop, i).wait()
        for kind in range(2):
            store_copy(kind, chunk).wait()


def exchange_call(sizes, est, obs, weight, offset, shot, gain, fit):
    parts, slabs, chunks, dirs, depth, width, share = sizes
    span = share * ROWS
    count = divisor(share // 2, PIECES)
    bf16 = jnp.bfloat16
    field = pltpu.VMEM((chunks, dirs, depth, ROWS, width), bf16)
    hops = pltpu.VMEM((chunks, parts - 1, 2 * depth, span, width), bf16)
    edge = pltpu.VMEM((chunks, depth, span, width), bf16)
    square = pltpu.VMEM((4 * depth * ROWS, 4 * depth * ROWS), bf16)
    smem = pl.BlockSpec(memory_space=pltpu.SMEM)
    hbm = pl.BlockSpec(memory_space=pl.ANY)
    dma = pltpu.SemaphoreType.DMA
    return pl.pallas_call(
        functools.partial(exchange_kernel, sizes),
        in_specs=[hbm, hbm, smem, smem, smem, smem, pl.BlockSpec(memory_space=pltpu.VMEM)],
        out_specs=hbm,
        out_shape=jax.ShapeDtypeStruct((2 * chunks, parts, depth, span, width), bf16),
        scratch_shapes=[field] * 6
        + [
            pltpu.VMEM((2 * depth, dirs * ROWS, width), bf16),
            square,
            square,
            pltpu.VMEM((parts * span, dirs * ROWS), bf16),
            pltpu.VMEM((2 * depth, span, width), jnp.float32),
            hops,
            hops,
            pltpu.VMEM((chunks, 2 * depth, span, width), bf16),
        ]
        + [edge] * 5
        + [
            dma((2, chunks)),
            dma((2, chunks)),
            dma((2, chunks, CUTS, 2)),
            dma((2, chunks, CUTS, 2)),
            dma((chunks, parts - 1, count, 2)),
            dma((2, chunks, count, 2)),
            dma((chunks, count, 2)),
            dma((2, chunks, parts - 1, count, 2)),
        ],
        compiler_params=pltpu.CompilerParams(
            collective_id=0, has_side_effects=True, vmem_limit_bytes=60 * 1024 * 1024
        ),
    )(est, obs, weight, offset, shot, gain, fit)


def synthesis_kernel(filtered, estimate, basis, correction, updated, wide):
    parts, depth, span, width = filtered.shape[1:]
    dirs = estimate.shape[0]
    part = lax.axis_index("dir").astype(jnp.int32)

    @pl.when(pl.program_id(0) == 0)
    def _():
        shape = (dirs * ROWS, basis.shape[1])
        spread = ones_where(iota(shape, 0) // ROWS + part * dirs == iota(shape, 1))
        narrow = against(spread, basis[...]).astype(jnp.bfloat16)
        shape = (parts * span, basis.shape[0])
        spread = ones_where(iota(shape, 0) // ROWS == iota(shape, 1))
        full = against(narrow, spread)
        wide[...] = jnp.where(same_row(full.shape), full, 0.0).astype(jnp.bfloat16)

    def one(j, carry):
        z = 2 * j
        columns = [
            jnp.concatenate([filtered[0, p, z + e] for p in range(parts)], axis=0) for e in range(2)
        ]
        made = jnp.dot(
            wide[...], jnp.concatenate(columns, axis=1), preferred_element_type=jnp.float32
        )
        for e in range(2):
            value = made[:, e * width : (e + 1) * width].reshape(dirs, ROWS, width)
            value = value.astype(jnp.bfloat16)
            correction[:, z + e] = value
            updated[:, z + e] = (
                estimate[:, z + e].astype(jnp.float32) + STEP_SIZE * value.astype(jnp.float32)
            ).astype(updated.dtype)
        return carry

    lax.fori_loop(0, depth // 2, one, 0)


def synthesis_call(filtered, estimate, basis):
    tiles, parts, depth, span, width = filtered.shape
    dirs = estimate.shape[0]
    place = pl.BlockSpec((dirs, depth, ROWS, width), lambda i: (0, 0, i, 0))
    shape = jax.ShapeDtypeStruct(estimate.shape, estimate.dtype)
    return pl.pallas_call(
        synthesis_kernel,
        grid=(tiles,),
        in_specs=[
            pl.BlockSpec((1, parts, depth, span, width), lambda i: (i, 0, 0, 0, 0)),
            place,
            pl.BlockSpec(basis.shape, lambda i: (0, 0)),
        ],
        out_specs=[place, place],
        out_shape=[shape, shape],
        scratch_shapes=[pltpu.VMEM((dirs * ROWS, parts * span), jnp.bfloat16)],
    )(filtered, estimate, basis)


def shards(
    estimate, observed, profile_weight, band_offset, slab_shot, shot_gain, fit_matrix, basis
):
    dirs, depth, rows, width = estimate.shape
    parts = lax.axis_size("dir")
    share = 2 * -(-fit_matrix.shape[1] // (2 * parts))
    sizes = (parts, lax.axis_size("gz"), rows // (2 * ROWS), dirs, depth, width, share)
    filtered = exchange_call(
        sizes, estimate, observed, profile_weight, band_offset, slab_shot, shot_gain, fit_matrix
    )
    return tuple(synthesis_call(filtered, estimate, basis))


def solution(mesh):
    return jax.shard_map(
        shards,
        mesh=mesh,
        in_specs=(
            P("dir", "gz", "gy", None),
            P("dir", "gz", "gy", None),
            P(),
            P(),
            P(),
            P(None, "dir"),
            P(),
            P(),
        ),
        out_specs=(P("dir", "gz", "gy", None), P("dir", "gz", "gy", None)),
        check_vma=False,
    )
```

profile of v0, /device:TPU:4, one launch (start us, length us, event | category | flops | bytes accessed | tf_op | source)
XLA Modules:
  0.0 222.8 jit_solution(4213029932432823772)
XLA Ops:
  0.6 1.4 copy.10.fit
  2.0 206.3 %shard_map.95.filtered = bf16[8,2,8,192,128]{4,3,2,1,0:T(8,128)(2,1)} custom-call(bf16[48,8,64,128]{3,2,1,0:T(8,128)(2,1)} %estimate.1, bf16[48,8,64,128]{3,2,1,0:T(8,128)(2,1)} %obs.1, f32[17]{0:T(128)} %weight.1, s32[17]{0:T(128)} %offset.1, s32[8]{0:T(128)} %shot.1, f32[4,48]{1,0:T(4,128)} %gain.1, bf16[96,45]{1,0:T(8,128)(2,1)} %copy.10.fit), custom_call_target="tpu_custom_call" | custom-call | tf_op jit(solution)/shard_map/pallas_call | solution.py:424
  208.4 14.4 %shard_map.96 = (bf16[48,8,64,128]{3,2,1,0:T(8,128)(2,1)}, bf16[48,8,64,128]{3,2,1,0:T(8,128)(2,1)}) custom-call(bf16[8,2,8,192,128]{4,3,2,1,0:T(8,128)(2,1)} %shard_map.95.filtered, bf16[48,8,64,128]{3,2,1,0:T(8,128)(2,1)} %estimate.1, bf16[45,96]{1,0:T(8,128)(2,1)} %basis.1), custom_call_target="tpu_custom_call" | custom-call | tf_op jit(solution)/shard_map/pallas_call | solution.py:497
where the time goes:
time: 225 us; the launch traced here: 223 us
  Pallas kernels  221 us (98%)
    pallas_call x1, Pallas kernels, exchange_call(): pl.pallas_call(functools.partial(exchange_kernel, sizes), in_specs=[hbm,...  206 us
    pallas_call x1, Pallas kernels, synthesis_call(): pl.pallas_call(synthesis_kernel, grid=(tiles,), in_specs=[pl.BlockSpec((1...  14.4 us

commit v1 on v0

--- a/solution.py
+++ b/solution.py
@@ -11,7 +11,7 @@
 STEP_SIZE = 0.5
 ROWS = 8
 PIECES = 4
-CUTS = 2
+CUTS = 4
 MESH = pl.DeviceIdType.MESH
 
 def divisor(count, most):
@@ -49,12 +49,18 @@
     total = jnp.where(same_row(shape), total, 0.0)
     high = total.astype(jnp.bfloat16)
     low = (total - high.astype(jnp.float32)).astype(jnp.bfloat16)
-    return jnp.concatenate([high, low], axis=0)
+    half = depth * ROWS
+    sides = [piece[o * half : (o + 1) * half] for o in range(2) for piece in (high, low)]
+    return jnp.concatenate(sides, axis=0)
+
+
+def both_parts(sums, half):
+    return sums[:half] + sums[half : 2 * half]
 
 
 def exchange_kernel(
     sizes, est, obs, weight, offset, shot, gain, fit, out,
-    est_kept, obs_kept, est_got, obs_got, far_a, far_b, res, band, band_back, fit_wide, own,
+    fit_kept, est_kept, obs_kept, est_got, obs_got, far_a, far_b, res, band, band_back, fit_wide, own,
     part_out, part_in, coef, coef_a, coef_b, mine, other, returned,
     load_sem, store_sem, pair_sem, far_sem, part_sem, edge_sem, back_sem, ret_sem,
 ):
@@ -67,7 +73,8 @@
     across = slab + 2 - 4 * odd
     has_away = jnp.logical_and(away >= 0, away < slabs)
     has_across = jnp.logical_and(across >= 0, across < slabs)
-    some = dirs // CUTS
+    cuts = divisor(dirs // 2, CUTS)
+    some = dirs // cuts
     span = share * ROWS
     count = divisor(share // 2, PIECES)
     step = span // count
@@ -138,10 +145,10 @@
             source.at[:, :, rows_at(odd, chunk), :], target.at[chunk], load_sem.at[kind, chunk]
         )
 
-    def part_copy(chunk, hop, i):
-        return remote(
-            part_out.at[chunk, hop - 1, :, piece(i), :], part_in.at[chunk, hop - 1, :, piece(i), :],
-            part_sem.at[chunk, hop - 1, i], "dir", part_of(hop),
+    def part_copy(o, chunk, hop, i):
+        at = (chunk, hop - 1, pl.ds(o * depth, depth), piece(i))
+        return remote(
+            part_out.at[at], part_in.at[at], part_sem.at[o, chunk, hop - 1, i], "dir", part_of(hop)
         )
 
     def edge_copy(kind, chunk, i):
@@ -177,12 +184,12 @@
 
     def begin(chunk):
         for kind in range(2):
-            for cut in range(CUTS):
+            for cut in range(cuts):
                 pair_copy(kind, chunk, cut).start()
 
         @pl.when(has_away)
         def _():
-            for cut in range(CUTS):
+            for cut in range(cuts):
                 away_copy(chunk, cut).start()
 
         for kind in range(2):
@@ -206,9 +213,12 @@
 
     shots = [shot[lax.div(index * depth, SLAB)] for index in (slab, partner)]
 
-    def residual(chunk, cut):
-        arrive(away_copy(chunk, cut), across_copy(chunk, cut))
-        pair_copy(1, chunk, cut).wait_recv()
+    def residual(o, chunk, cut):
+        if o:
+            pair_copy(1, chunk, cut).wait_recv()
+        else:
+            arrive(away_copy(chunk, cut), across_copy(chunk, cut))
+        seen = (obs_kept, obs_got)[o]
 
         def one(j, carry):
             d = cut * some + 2 * j
@@ -220,27 +230,26 @@
                 ]
                 columns.append(jnp.concatenate(planes, axis=0))
             wide = jnp.concatenate(columns, axis=1).astype(jnp.bfloat16)
-            sums = jnp.dot(band[...], wide, preferred_element_type=jnp.float32)
-            sums = sums[: 2 * half] + sums[2 * half :]
-            for o, seen in enumerate((obs_kept, obs_got)):
-                values = []
-                for e in range(2):
-                    scale = gain[shots[o], d + e]
-                    blurred = sums[o * half : (o + 1) * half, e * width : (e + 1) * width]
-                    value = seen[chunk, d + e].astype(jnp.float32).reshape(half, width)
-                    values.append(scale * (value - scale * blurred))
-                at = pl.ds(pl.multiple_of(d * ROWS, pair_rows), pair_rows)
-                for z in range(depth):
-                    cut_rows = slice(z * ROWS, (z + 1) * ROWS)
-                    both = jnp.concatenate([value[cut_rows] for value in values], axis=0)
-                    res[o * depth + z, at, :] = both.astype(jnp.bfloat16)
+            rows = band[2 * o * half : 2 * (o + 1) * half, :]
+            sums = both_parts(jnp.dot(rows, wide, preferred_element_type=jnp.float32), half)
+            values = []
+            for e in range(2):
+                scale = gain[shots[o], d + e]
+                value = seen[chunk, d + e].astype(jnp.float32).reshape(half, width)
+                value = value - scale * sums[:, e * width : (e + 1) * width]
+                values.append(scale * value)
+            at = pl.ds(pl.multiple_of(d * ROWS, pair_rows), pair_rows)
+            for z in range(depth):
+                cut_rows = slice(z * ROWS, (z + 1) * ROWS)
+                both = jnp.concatenate([value[cut_rows] for value in values], axis=0)
+                res[o * depth + z, at, :] = both.astype(jnp.bfloat16)
             return carry
 
         lax.fori_loop(0, some // 2, one, 0)
 
-    def fitting(chunk):
+    def fitting(o, chunk):
         def one(j, carry):
-            z = 2 * j
+            z = o * depth + 2 * j
             wide = jnp.concatenate([res[z], res[z + 1]], axis=1)
             made = jnp.dot(fit_wide[...], wide, preferred_element_type=jnp.float32)
             for e in range(2):
@@ -251,14 +260,14 @@
                     part_out[chunk, hop - 1, z + e] = piece_of.astype(jnp.bfloat16)
             return carry
 
-        lax.fori_loop(0, depth, one, 0)
+        lax.fori_loop(0, depth // 2, one, 0)
         for i in range(count):
             for hop in range(1, parts):
-                part_copy(chunk, hop, i).start()
-
-    def gather(chunk, i):
+                part_copy(o, chunk, hop, i).start()
+
+    def gather(o, chunk, i):
         for hop in range(1, parts):
-            part_copy(chunk, hop, i).wait_recv()
+            part_copy(o, chunk, hop, i).wait_recv()
 
         def one(z, carry):
             value = own[z, piece(i), :]
@@ -267,15 +276,11 @@
             coef[chunk, z, piece(i), :] = value.astype(jnp.bfloat16)
             return carry
 
-        lax.fori_loop(0, 2 * depth, one, 0)
-
-        @pl.when(has_away)
+        lax.fori_loop(o * depth, (o + 1) * depth, one, 0)
+
+        @pl.when((has_away, has_across)[o])
         def _():
-            edge_copy(0, chunk, i).start()
-
-        @pl.when(has_across)
-        def _():
-            edge_copy(1, chunk, i).start()
+            edge_copy(o, chunk, i).start()
 
     def smooth(chunk, i):
         arrive(edge_copy(0, chunk, i), edge_copy(1, chunk, i))
@@ -292,10 +297,10 @@
             ]
             wide = jnp.concatenate(columns, axis=1).astype(jnp.bfloat16)
             sums = jnp.dot(band_back[...], wide, preferred_element_type=jnp.float32)
-            sums = sums[: 2 * half] + sums[2 * half :]
             for o, ref in enumerate((mine, other)):
+                side = both_parts(sums[2 * o * half : 2 * (o + 1) * half], half)
                 for z in range(depth):
-                    value = sums[o * half + z * ROWS : o * half + (z + 1) * ROWS]
+                    value = side[z * ROWS : (z + 1) * ROWS]
                     both = jnp.concatenate([value[:, :width], value[:, width:]], axis=0)
                     ref[chunk, z, at, :] = both.astype(jnp.bfloat16)
             return carry
@@ -310,6 +315,8 @@
         for hop in range(1, parts):
             ret_copy(1, chunk, hop, i).start()
 
+    fit_copy = pltpu.make_async_copy(fit, fit_kept, load_sem.at[2, 0])
+    fit_copy.start()
     begin(0)
     if chunks > 1:
         begin(1)
@@ -336,32 +343,38 @@
 
     band[...] = band_matrix(weight, offset, odd, depth, 1)
     band_back[...] = band_matrix(weight, offset, odd, depth, -1)
-    line = iota((parts * span, fit.shape[1]), 0) // ROWS
+    line = iota((parts * span, fit.shape[0]), 0) // ROWS
     chosen = lax.rem(line // share + part, parts) * share + lax.rem(line, share)
     spread = ones_where(chosen == iota(line.shape, 1))
-    narrow = against(spread, fit[...]).astype(jnp.bfloat16)
-    shape = (dirs * ROWS, fit.shape[0])
+    fit_copy.wait()
+    narrow = jnp.dot(spread, fit_kept[...], preferred_element_type=jnp.float32).astype(jnp.bfloat16)
+    shape = (dirs * ROWS, fit.shape[1])
     spread = ones_where(iota(shape, 0) // ROWS + part * dirs == iota(shape, 1))
     full = against(narrow, spread)
     fit_wide[...] = jnp.where(same_row(full.shape), full, 0.0).astype(jnp.bfloat16)
 
-    for cut in range(CUTS):
+    for cut in range(cuts):
         forward(0, cut)
     for chunk in range(chunks):
         more = chunk + 1 < chunks
         for kind in range(2):
             load_copy(kind, chunk).wait()
-        for cut in range(CUTS):
-            residual(chunk, cut)
-        fitting(chunk)
+        for cut in range(cuts):
+            residual(0, chunk, cut)
+        fitting(0, chunk)
+        for cut in range(cuts):
+            residual(1, chunk, cut)
+        fitting(1, chunk)
         if chunk:
             for i in range(count):
                 pass_on(chunk - 1, i)
             store_copy(1, chunk - 1).start()
         for i in range(count):
-            gather(chunk, i)
-            for cut in range(CUTS):
-                if more and cut * count // CUTS == i:
+            gather(0, chunk, i)
+        for i in range(count):
+            gather(1, chunk, i)
+            for cut in range(cuts):
+                if more and cut * count // cuts == i:
                     forward(chunk + 1, cut)
             if i:
                 smooth(chunk, i - 1)
@@ -377,7 +390,7 @@
             begin(chunk + 2)
 
     for chunk in range(chunks):
-        for cut in range(CUTS):
+        for cut in range(cuts):
             for kind in range(2):
                 pair_copy(kind, chunk, cut).wait_send()
 
@@ -391,7 +404,8 @@
 
         for i in range(count):
             for hop in range(1, parts):
-                part_copy(chunk, hop, i).wait_send()
+                for o in range(2):
+                    part_copy(o, chunk, hop, i).wait_send()
 
             @pl.when(has_away)
             def _(chunk=chunk, i=i):
@@ -413,6 +427,7 @@
     parts, slabs, chunks, dirs, depth, width, share = sizes
     span = share * ROWS
     count = divisor(share // 2, PIECES)
+    cuts = divisor(dirs // 2, CUTS)
     bf16 = jnp.bfloat16
     field = pltpu.VMEM((chunks, dirs, depth, ROWS, width), bf16)
     hops = pltpu.VMEM((chunks, parts - 1, 2 * depth, span, width), bf16)
@@ -423,10 +438,11 @@
     dma = pltpu.SemaphoreType.DMA
     return pl.pallas_call(
         functools.partial(exchange_kernel, sizes),
-        in_specs=[hbm, hbm, smem, smem, smem, smem, pl.BlockSpec(memory_space=pltpu.VMEM)],
+        in_specs=[hbm, hbm, smem, smem, smem, smem, hbm],
         out_specs=hbm,
         out_shape=jax.ShapeDtypeStruct((2 * chunks, parts, depth, span, width), bf16),
-        scratch_shapes=[field] * 6
+        scratch_shapes=[pltpu.VMEM(fit.shape[::-1], bf16)]
+        + [field] * 6
         + [
             pltpu.VMEM((2 * depth, dirs * ROWS, width), bf16),
             square,
@@ -439,11 +455,11 @@
         ]
         + [edge] * 5
         + [
+            dma((3, chunks)),
             dma((2, chunks)),
-            dma((2, chunks)),
-            dma((2, chunks, CUTS, 2)),
-            dma((2, chunks, CUTS, 2)),
-            dma((chunks, parts - 1, count, 2)),
+            dma((2, chunks, cuts, 2)),
+            dma((2, chunks, cuts, 2)),
+            dma((2, chunks, parts - 1, count, 2)),
             dma((2, chunks, count, 2)),
             dma((chunks, count, 2)),
             dma((2, chunks, parts - 1, count, 2)),
@@ -451,7 +467,7 @@
         compiler_params=pltpu.CompilerParams(
             collective_id=0, has_side_effects=True, vmem_limit_bytes=60 * 1024 * 1024
         ),
-    )(est, obs, weight, offset, shot, gain, fit)
+    )(est, obs, weight, offset, shot, gain, fit.T)
 
 
 def synthesis_kernel(filtered, estimate, basis, correction, updated, wide):

time: 225 us -> 215 us (0.956)
  Pallas kernels: 221 us -> 214 us
    pallas_call x1, Pallas kernels: 206 us -> 199 us  [exchange_call(): pl.pallas_call(functools.partial(exchange_kernel, sizes), in_specs=[hbm,...]
where the time goes in v1:
time: 215 us; the launch traced here: 214 us
  Pallas kernels  214 us (100%)
    pallas_call x1, Pallas kernels, exchange_call(): pl.pallas_call(functools.partial(exchange_kernel, sizes), in_specs=[hbm,...  199 us
    pallas_call x1, Pallas kernels, synthesis_call(): pl.pallas_call(synthesis_kernel, grid=(tiles,), in_specs=[pl.BlockSpec((1...  14.4 us

profile of v1, /device:TPU:4, one launch (start us, length us, event | category | flops | bytes accessed | tf_op | source)
XLA Modules:
  0.0 214.5 jit_solution(10482523525182393757)
XLA Ops:
  0.6 199.5 %shard_map.95.filtered = bf16[8,2,8,192,128]{4,3,2,1,0:T(8,128)(2,1)} custom-call(bf16[48,8,64,128]{3,2,1,0:T(8,128)(2,1)} %estimate.1, bf16[48,8,64,128]{3,2,1,0:T(8,128)(2,1)} %obs.1, f32[17]{0:T(128)} %weight.1, s32[17]{0:T(128)} %offset.1, s32[8]{0:T(128)} %shot.1, f32[4,48]{1,0:T(4,128)} %gain.1, bf16[45,96]{1,0:T(8,128)(2,1)} %bitcast.1), custom_call_target="tpu_custom_call" | custom-call | tf_op jit(solution)/shard_map/pallas_call | solution.py:439
  200.1 14.4 %shard_map.96 = (bf16[48,8,64,128]{3,2,1,0:T(8,128)(2,1)}, bf16[48,8,64,128]{3,2,1,0:T(8,128)(2,1)}) custom-call(bf16[8,2,8,192,128]{4,3,2,1,0:T(8,128)(2,1)} %shard_map.95.filtered, bf16[48,8,64,128]{3,2,1,0:T(8,128)(2,1)} %estimate.1, bf16[45,96]{1,0:T(8,128)(2,1)} %basis.1), custom_call_target="tpu_custom_call" | custom-call | tf_op jit(solution)/shard_map/pallas_call | solution.py:513

commit v2 on v1

--- a/solution.py
+++ b/solution.py
@@ -59,7 +59,7 @@
 
 
 def exchange_kernel(
-    sizes, est, obs, weight, offset, shot, gain, fit, out,
+    sizes, est, obs, weight, offset, shot, gain, fit, out, final,
     fit_kept, est_kept, obs_kept, est_got, obs_got, far_a, far_b, res, band, band_back, fit_wide, own,
     part_out, part_in, coef, coef_a, coef_b, mine, other, returned,
     load_sem, store_sem, pair_sem, far_sem, part_sem, edge_sem, back_sem, ret_sem,
@@ -177,6 +177,8 @@
         )
 
     def store_copy(kind, chunk):
+        if kind and chunk == chunks - 1:
+            return pltpu.make_async_copy(returned.at[chunk], final, store_sem.at[kind, chunk])
         source = (mine, returned)[kind]
         return pltpu.make_async_copy(
             source.at[chunk], out.at[tile_of(kind, chunk), part], store_sem.at[kind, chunk]
@@ -313,7 +315,8 @@
     def pass_on(chunk, i):
         back_copy(chunk, i).wait_recv()
         for hop in range(1, parts):
-            ret_copy(1, chunk, hop, i).start()
+            if chunk < chunks - 1:
+                ret_copy(1, chunk, hop, i).start()
 
     fit_copy = pltpu.make_async_copy(fit, fit_kept, load_sem.at[2, 0])
     fit_copy.start()
@@ -418,7 +421,8 @@
             back_copy(chunk, i).wait_send()
             for kind in range(2):
                 for hop in range(1, parts):
-                    ret_copy(kind, chunk, hop, i).wait()
+                    if kind == 0 or chunk < chunks - 1:
+                        ret_copy(kind, chunk, hop, i).wait()
         for kind in range(2):
             store_copy(kind, chunk).wait()
 
@@ -439,8 +443,11 @@
     return pl.pallas_call(
         functools.partial(exchange_kernel, sizes),
         in_specs=[hbm, hbm, smem, smem, smem, smem, hbm],
-        out_specs=hbm,
-        out_shape=jax.ShapeDtypeStruct((2 * chunks, parts, depth, span, width), bf16),
+        out_specs=[hbm, hbm],
+        out_shape=[
+            jax.ShapeDtypeStruct((2 * chunks, parts, depth, span, width), bf16),
+            jax.ShapeDtypeStruct((depth, span, width), bf16),
+        ],
         scratch_shapes=[pltpu.VMEM(fit.shape[::-1], bf16)]
         + [field] * 6
         + [
@@ -470,8 +477,9 @@
     )(est, obs, weight, offset, shot, gain, fit.T)
 
 
-def synthesis_kernel(filtered, estimate, basis, correction, updated, wide):
-    parts, depth, span, width = filtered.shape[1:]
+def synthesis_kernel(by_hop, filtered, estimate, basis, *refs):
+    correction, updated, wide = refs[-3:]
+    parts, depth, span, width = filtered.shape[-4:]
     dirs = estimate.shape[0]
     part = lax.axis_index("dir").astype(jnp.int32)
 
@@ -481,7 +489,11 @@
         spread = ones_where(iota(shape, 0) // ROWS + part * dirs == iota(shape, 1))
         narrow = against(spread, basis[...]).astype(jnp.bfloat16)
         shape = (parts * span, basis.shape[0])
-        spread = ones_where(iota(shape, 0) // ROWS == iota(shape, 1))
+        line = iota(shape, 0) // ROWS
+        if by_hop:
+            share = span // ROWS
+            line = lax.rem(part - line // share + parts, parts) * share + lax.rem(line, share)
+        spread = ones_where(line == iota(shape, 1))
         full = against(narrow, spread)
         wide[...] = jnp.where(same_row(full.shape), full, 0.0).astype(jnp.bfloat16)
 
@@ -505,23 +517,65 @@
     lax.fori_loop(0, depth // 2, one, 0)
 
 
+def final_kernel(*refs):
+    pieces, rest = refs[: -8], refs[-8:]
+    estimate, basis, _, _, correction, updated, wide, joined = rest
+    for number, piece in enumerate(pieces):
+        joined[0, number] = piece[...]
+    synthesis_kernel(True, joined, estimate, basis, correction, updated, wide)
+
+
+def final_tile(tiles):
+    odd = lax.rem(lax.axis_index("gz").astype(jnp.int32), 2)
+    return (1 - odd) * (tiles // 2) + tiles // 2 - 1
+
+
 def synthesis_call(filtered, estimate, basis):
     tiles, parts, depth, span, width = filtered.shape
     dirs = estimate.shape[0]
-    place = pl.BlockSpec((dirs, depth, ROWS, width), lambda i: (0, 0, i, 0))
+
+    def tile(i):
+        return i + (i >= final_tile(tiles)).astype(jnp.int32)
+
+    place = pl.BlockSpec((dirs, depth, ROWS, width), lambda i: (0, 0, tile(i), 0))
     shape = jax.ShapeDtypeStruct(estimate.shape, estimate.dtype)
     return pl.pallas_call(
-        synthesis_kernel,
-        grid=(tiles,),
+        functools.partial(synthesis_kernel, False),
+        grid=(tiles - 1,),
         in_specs=[
-            pl.BlockSpec((1, parts, depth, span, width), lambda i: (i, 0, 0, 0, 0)),
+            pl.BlockSpec((1, parts, depth, span, width), lambda i: (tile(i), 0, 0, 0, 0)),
             place,
             pl.BlockSpec(basis.shape, lambda i: (0, 0)),
         ],
         out_specs=[place, place],
         out_shape=[shape, shape],
         scratch_shapes=[pltpu.VMEM((dirs * ROWS, parts * span), jnp.bfloat16)],
+        cost_estimate=pl.CostEstimate(
+            flops=2 * parts * span * estimate.size, bytes_accessed=8 * estimate.size, transcendentals=0
+        ),
     )(filtered, estimate, basis)
+
+
+def final_call(pieces, estimate, basis, made, tiles):
+    depth, span, width = pieces[0].shape
+    dirs = estimate.shape[0]
+    place = pl.BlockSpec((dirs, depth, ROWS, width), lambda i: (0, 0, final_tile(tiles), 0))
+    shape = jax.ShapeDtypeStruct(estimate.shape, estimate.dtype)
+    parts = len(pieces)
+    hbm = pl.BlockSpec(memory_space=pl.ANY)
+    return pl.pallas_call(
+        final_kernel,
+        grid=(1,),
+        in_specs=[pl.BlockSpec(pieces[0].shape, lambda i: (0, 0, 0))] * parts
+        + [place, pl.BlockSpec(basis.shape, lambda i: (0, 0)), hbm, hbm],
+        out_specs=[place, place],
+        out_shape=[shape, shape],
+        scratch_shapes=[
+            pltpu.VMEM((dirs * ROWS, parts * span), jnp.bfloat16),
+            pltpu.VMEM((1, parts, depth, span, width), jnp.bfloat16),
+        ],
+        input_output_aliases={parts + 2: 0, parts + 3: 1},
+    )(*pieces, estimate, basis, *made)
 
 
 def shards(
@@ -531,10 +585,15 @@
     parts = lax.axis_size("dir")
     share = 2 * -(-fit_matrix.shape[1] // (2 * parts))
     sizes = (parts, lax.axis_size("gz"), rows // (2 * ROWS), dirs, depth, width, share)
-    filtered = exchange_call(
+    filtered, last = exchange_call(
         sizes, estimate, observed, profile_weight, band_offset, slab_shot, shot_gain, fit_matrix
     )
-    return tuple(synthesis_call(filtered, estimate, basis))
+    pieces = [last] + [
+        lax.ppermute(last, "dir", [(i, (i + hop) % parts) for i in range(parts)])
+        for hop in range(1, parts)
+    ]
+    made = synthesis_call(filtered, estimate, basis)
+    return tuple(final_call(pieces, estimate, basis, made, filtered.shape[0]))
 
 
 def solution(mesh):

time: 215 us -> 211 us (0.981)
  Pallas kernels: 214 us -> 208 us
    pallas_call x1, Pallas kernels: 199 us -> 191 us  [exchange_call(): pl.pallas_call(functools.partial(exchange_kernel, sizes), in_specs=[hbm,...]
    pallas_call x1 -> x2, Pallas kernels: 14.4 us -> 17.1 us  [the longest x1 13.1 us: synthesis_call(): pl.pallas_call(functools.partial(synthesis_kernel, False), grid=(tiles -...]
  transfers between devices with their start and end apart: 0 -> 1, of which waited for: 0 -> 0; matrix products, arithmetic and copies ran while one was open for 0% -> 0% of each run, Pallas kernels for 0% -> 6%
where the time goes in v2:
time: 211 us
  Pallas kernels  208 us (99%)
    pallas_call x1, Pallas kernels, exchange_call(): pl.pallas_call(functools.partial(exchange_kernel, sizes), in_specs=[hbm,...  191 us
    pallas_call x1, Pallas kernels, synthesis_call(): pl.pallas_call(functools.partial(synthesis_kernel, False), grid=(tiles -...  13.1 us
  transfers between devices with their start and end apart: 1, of which 0 were waited for; matrix products, arithmetic and copies ran while one was open for 0% of the time, Pallas kernels for 6%

profile of v2, /device:TPU:4, one launch (start us, length us, event | category | flops | bytes accessed | tf_op | source)
XLA Modules:
  0.0 210.7 jit_solution(18435825257846151463)
XLA Ops:
  0.6 191.0 %shard_map.95 = (bf16[8,2,8,192,128]{4,3,2,1,0:T(8,128)(2,1)}, bf16[8,192,128]{2,1,0:T(8,128)(2,1)}) custom-call(bf16[48,8,64,128]{3,2,1,0:T(8,128)(2,1)} %refs_2_.1, bf16[48,8,64,128]{3,2,1,0:T(8,128)(2,1)} %obs.1, f32[17]{0:T(128)} %weight.1, s32[17]{0:T(128)} %offset.1, s32[8]{0:T(128)} %shot.1, f32[4,48]{1,0:T(4,128)} %gain.1, bf16[45,96]{1,0:T(8,128)(2,1)} %bitcast.1), custom_call_target="tpu_custom_call" | custom-call | tf_op jit(solution)/shard_map/pallas_call | solution.py:443
  191.7 1.1 collective-permute-start
  192.8 13.1 %shard_map.96 = (bf16[48,8,64,128]{3,2,1,0:T(8,128)(2,1)}, bf16[48,8,64,128]{3,2,1,0:T(8,128)(2,1)}) custom-call(bf16[8,2,8,192,128]{4,3,2,1,0:T(8,128)(2,1)} %get-tuple-element.7.filtered, bf16[48,8,64,128]{3,2,1,0:T(8,128)(2,1)} %refs_2_.1, bf16[45,96]{1,0:T(8,128)(2,1)} %refs_3_.1), custom_call_target="tpu_custom_call" | custom-call | flops 2415919104 | bytes 25165824 | tf_op jit(solution)/shard_map/pallas_call | solution.py:542
  205.9 0.0 collective-permute-done.refs_1_
  205.9 0.0 copy-start
  205.9 0.7 copy-done
  206.6 4.0 %shard_map.97 = (bf16[48,8,64,128]{3,2,1,0:T(8,128)(2,1)}, bf16[48,8,64,128]{3,2,1,0:T(8,128)(2,1)}) custom-call(bf16[8,192,128]{2,1,0:T(8,128)(2,1)} %get-tuple-element.6.refs_0_, bf16[8,192,128]{2,1,0:T(8,128)(2,1)} %copy-done, bf16[48,8,64,128]{3,2,1,0:T(8,128)(2,1)} %refs_2_.1, ...), custom_call_target="tpu_custom_call", output_to_operand_aliasing={{0}: (4, {}), {1}: (5, {})} | custom-call | tf_op jit(solution)/shard_map/pallas_call | solution.py:566
Async XLA Ops:
  191.7 14.2 %collective-permute-start = (bf16[8,192,128]{2,1,0:T(8,128)(2,1)}, bf16[8,192,128]{2,1,0:T(8,128)(2,1)S(1)}, u32[]{:S(2)}, u32[]{:S(2)}) collective-permute-start(bf16[8,192,128]{2,1,0:T(8,128)(2,1)} %get-tuple-element.6.refs_0_), channel_id=1, source_target_pairs={{0,16},{16,0},{1,17},{17,1},{2,18},{18,2},{3,19},{19,3},{4,20},{20... | collective-permute-start | bytes 1179656 | tf_op jit(solution)/shard_map/ppermute | solution.py:592
  205.9 0.8 copy-start
